TPU v7x, 256 devices: a whole 4x4x8 slice. The times are simulated.
256 devices in a mesh: lon: 32 (over y, z), lat: 8 (over x, core).
Axes of the slice: x: 4, y: 4, z: 8, core: 2. Of those that a mesh axis runs over, the one named last changes fastest.
Arguments:
- height: float32 [1024, 512, 1024], P(None, 'lon', 'lat'), may hold values from -1 to 1
- land_sea: int32 [512, 1024], P('lon', 'lat'), may hold values 0 or 1
- patterns: bfloat16 [512, 2, 512, 1024], P(None, None, 'lon', 'lat'), may hold values from -0.01171875 to 0.01171875
Outputs:
- covariance: float32 [32, 512, 512], P('lon', 'lat')
All inputs are finite; a program needn't handle non-finite values. No bound on the sum of `land_sea` on one device may be relied on, other than what follows from the above.
Results may differ from a plain program's by a relative error of at most 0.0003.
The roundings to bfloat16 on the way count: a program that leaves them out, or rounds other values in their place, can miss the bound.
Values sent between devices are 32-bit elements; how exact they have to be, the bound alone decides.
A program may use at most 128 MiB of HBM per device.

v0:
```python
import math
import jax
import jax.numpy as jnp
from jax import lax
from jax.sharding import PartitionSpec as P

LAG_DEV = 1
GRAVITY = 9.81
ROTATION = 7.2921e-05
EARTH_RADIUS = 6371000.0
LAT_SOUTH = 20.0
LAT_SPAN = 45.0
LON_STEP = 1.0 / 12.0


def padded_2(shard, sides, width):
    for axis, dim in sides:
        devices, length = (lax.axis_size(axis), shard.shape[dim])
        up = [(i, (i + 1) % devices) for i in range(devices - 1)]
        down = [(j, i) for i, j in up]
        last = lax.slice_in_dim(shard, length - width, length, axis=dim)
        initial = lax.slice_in_dim(shard, 0, width, axis=dim)
        before = lax.ppermute(last, axis, up)
        after = lax.ppermute(initial, axis, down)
        shard = jnp.concatenate([before, shard, after], axis=dim)
    return shard


def stencil_coefs(rows_index, total_rows):
    degrees = LAT_SOUTH + LAT_SPAN * (rows_index.astype(jnp.float32) + 0.5) / total_rows
    radians = degrees * (math.pi / 180.0)
    coriolis = 2.0 * ROTATION * jnp.sin(radians)
    north_step = EARTH_RADIUS * (LAT_SPAN / total_rows) * (math.pi / 180.0)
    east_step = EARTH_RADIUS * jnp.cos(radians) * (LON_STEP * math.pi / 180.0)
    return (-GRAVITY / (coriolis * 2.0 * north_step), GRAVITY / (coriolis * 2.0 * east_step))


def velocities(padded, coef_east, coef_north, ocean):
    lat_diff = padded[:, 1:-1, 2:] - padded[:, 1:-1, :-2]
    lon_diff = padded[:, 2:, 1:-1] - padded[:, :-2, 1:-1]
    return (coef_east * lat_diff * ocean, coef_north * lon_diff * ocean)


def on_device(height, land_sea, patterns):
    days, lon_cells, lat_cells = height.shape
    lat_devices = lax.axis_size("lat")
    lon_devices = lax.axis_size("lon")
    total_rows = lat_cells * lat_devices
    lat_place = lax.axis_index("lat")
    lon_place = lax.axis_index("lon")
    rows_index = lat_place * lat_cells + jnp.arange(lat_cells, dtype=jnp.int32)
    coef_east, coef_north = stencil_coefs(rows_index, total_rows)
    ocean = land_sea.astype(jnp.float32)
    padded = padded_2(height, (("lon", 1), ("lat", 2)), 1)
    east_vel, north_vel = velocities(padded, coef_east, coef_north, ocean)
    local_energy = jnp.sum(east_vel * east_vel + north_vel * north_vel)
    stacked = (
        jnp.stack([east_vel, north_vel], axis=1)
        .astype(jnp.bfloat16)
        .reshape(days, 2 * lon_cells * lat_cells)
    )
    mode_count = patterns.shape[0]
    owned = mode_count // lat_devices
    flat_patterns = patterns.reshape(mode_count, 2 * lon_cells * lat_cells)
    energy = lax.psum(local_energy, ("lon", "lat"))
    totals = lax.psum(
        lax.dot_general(
            flat_patterns, stacked, (((1,), (1,)), ((), ())), preferred_element_type=jnp.float32
        ),
        ("lon", "lat"),
    )
    cell_total = 2.0 * days * lon_cells * lon_devices * total_rows
    centered = totals - jnp.mean(totals, axis=1, keepdims=True)
    normed = centered / jnp.sqrt(energy / cell_total + 1e-06)
    my_rows = lax.dynamic_slice_in_dim(normed, lat_place * owned, owned, 0)
    padded_rows = jnp.concatenate([my_rows, jnp.zeros_like(my_rows)], axis=1)
    lag = lon_place * LAG_DEV + 0
    shifted = lax.dynamic_slice_in_dim(padded_rows, lag, days, 1)
    product = lax.dot_general(
        shifted,
        normed,
        (((1,), (1,)), ((), ())),
        precision=lax.Precision.HIGHEST,
        preferred_element_type=jnp.float32,
    )
    results = [product / (days - lag).astype(jnp.float32)]
    return jnp.stack(results, axis=0)


def solution(mesh):
    placed = (P(None, "lon", "lat"), P("lon", "lat"), P(None, None, "lon", "lat"))
    return jax.shard_map(
        on_device, mesh=mesh, in_specs=placed, out_specs=P("lon", "lat", None), check_vma=False
    )
```

profile of v0, /device:TPU:2, one launch (start us, length us, event | category | flops | bytes accessed | tf_op | source)
XLA Modules:
  0.0 381.3 jit_solution(7635947852473987990)
XLA Ops:
  6.5 0.0 copy-start.2
  6.5 0.0 all-reduce.3.cloned.1.call-start
  6.5 6.1 %copy.10 = f32[1024,16,128]{2,0,1:T(8,128)S(1)} copy(f32[1024,16,128]{2,1,0:T(8,128)} %param.3) | data formatting | bytes 16777216 | tf_op args[0]
  12.6 0.0 copy-start.1
  12.6 3.3 copy-done.1
  15.9 0.1 fusion.23
  16.0 3.9 %collective-permute-start = (f32[1024,1,128]{2,0,1:T(8,128)S(1)}, f32[1024,1,128]{2,0,1:T(8,128)S(1)}, u32[]{:S(2)}, u32[]{:S(2)}) collective-permute-start(f32[1024,1,128]{2,0,1:T(8,128)S(1)} %get-tuple-element.11), channel_id=1, source_target_pairs={{0,8},{8,16},{16,24},{24,32},{32,40},{40,48},{48,56},{56,64},{64,7... | collective-permute-start | bytes 1572872 | tf_op jit(solution)/shard_map/ppermute | solution.py:23
  19.9 1.3 collective-permute-start.1
  21.2 0.0 copy-done.2
  21.2 9.8 %collective-permute-done = f32[1024,1,128]{2,0,1:T(8,128)S(1)} collective-permute-done((f32[1024,1,128]{2,0,1:T(8,128)S(1)}, f32[1024,1,128]{2,0,1:T(8,128)S(1)}, u32[]{:S(2)}, u32[]{:S(2)}) %collective-permute-start) | collective-permute-done | bytes 524320 | tf_op jit(solution)/shard_map/ppermute | solution.py:23
  31.0 5.8 %constant_dynamic-update-slice_fusion.1 = f32[1024,18,128]{2,0,1:T(8,128)S(1)} fusion(f32[1024,18,128]{2,0,1:T(8,128)S(1)} %constant_dynamic-update-slice_fusion.2, f32[1024,16,128]{2,1,0:T(8,128)} %param.3), kind=kLoop, calls=%fused_computation.24 | loop fusion | bytes 16777216
  36.8 0.0 collective-permute-done.1
  36.9 0.0 copy-start
  36.9 8.4 %fusion.22 = (f32[1024,18,1]{2,0,1:T(8,128)}, f32[1024,18,1]{2,0,1:T(8,128)}) fusion(f32[1024,18,128]{2,0,1:T(8,128)S(1)} %constant_dynamic-update-slice_fusion), kind=kLoop, calls=%fused_computation.35 | loop fusion | bytes 294912 | tf_op jit(solution)/shard_map/slice | solution.py:22
  45.3 0.9 copy-done
  46.2 5.6 %copy.13 = f32[1024,18,1]{0,2,1:T(1,128)S(1)} copy(f32[1024,18,1]{2,0,1:T(8,128)} %get-tuple-element.8) | data formatting | bytes 147456 | tf_op jit(solution)/shard_map/slice | solution.py:22
  51.8 1.9 collective-permute-start.2
  53.7 5.6 %copy.15 = f32[1024,18,1]{0,2,1:T(1,128)S(1)} copy(f32[1024,18,1]{2,0,1:T(8,128)} %get-tuple-element.9) | data formatting | bytes 147456 | tf_op jit(solution)/shard_map/slice | solution.py:21
  59.3 2.6 collective-permute-start.3
  61.9 0.1 multiply_divide_fusion
  62.0 0.0 collective-permute-done.2
  62.0 5.1 %copy.14 = f32[1024,18,1]{2,0,1:T(8,128)} copy(f32[1024,18,1]{0,2,1:T(1,128)S(1)} %collective-permute-done.2) | data formatting | bytes 147456 | tf_op jit(solution)/shard_map/ppermute | solution.py:24
  67.1 0.0 collective-permute-done.3
  67.1 5.2 %copy.16 = f32[1024,18,1]{2,0,1:T(8,128)} copy(f32[1024,18,1]{0,2,1:T(1,128)S(1)} %collective-permute-done.3) | data formatting | bytes 147456 | tf_op jit(solution)/shard_map/ppermute | solution.py:23
  72.2 18.3 %add_reduce_fusion = (f32[]{:T(128)}, bf16[1024,16,128]{2,0,1:T(8,128)(2,1)S(1)}, bf16[1024,1,16,128]{3,0,2,1:T(8,128)(2,1)S(1)}) fusion(f32[16,128]{1,0:T(8,128)S(1)} %convert_element_type.18, f32[1024,16,128]{2,0,1:T(8,128)} %copy-done.1, f32[1024,1,128]{2,0,1:T(8,128)S(1)} %collective-permute-done, f32[1024,1,128]{2,0,1:T(8,128)S(1)} %collective-permute-done.1, ...), kind=kLoop, calls=%fused_computation.14 | loop fusion | flops 33554432 | bytes 27419652 | tf_op jit(solution)/shard_map/reduce_sum | solution.py:56
  90.5 8.1 %fusion.11 = f32[512,1024]{0,1:T(8,128)} fusion(bf16[512,2,16,128]{3,2,1,0:T(8,128)(2,1)} %param.5, bf16[1024,1,16,128]{3,0,2,1:T(8,128)(2,1)S(1)} %get-tuple-element.7, bf16[1024,1,16,128]{3,0,2,1:T(8,128)(2,1)S(1)} %bitcast.14), kind=kOutput, calls=%fused_computation.19 | convolution fusion | flops 4299161600 | bytes 14680064 | tf_op jit(solution)/shard_map/dot_general | solution.py:67
  98.6 0.0 all-reduce.3.cloned.1.call-update
  98.7 80.3 %psum.15 = f32[]{:T(128)} all-reduce(f32[]{:T(128)} %get-tuple-element.5), channel_id=1, replica_groups=mesh['lon'=32,'lat'=8] {'lon','lat'}, use_global_device_ids=true, to_apply=%region_3.0 | all-reduce | flops 1 | bytes 8 | tf_op jit(solution)/shard_map/psum | solution.py:65
  179.7 188.9 %all-reduce.3.cloned.1.call-done = f32[512,1024]{0,1:T(8,128)} async-done(((f32[512,1024]{0,1:T(8,128)}), f32[512,1024]{0,1:T(8,128)}) %all-reduce.3.cloned.1.call-update) | async-done | bytes 2097168 | tf_op jit(solution)/shard_map/psum | solution.py:66
  368.6 1.8 reduce_sum.18
  370.4 1.9 subtract_divide_fusion
  372.2 0.2 constant_dynamic-slice_fusion
  372.4 2.0 fusion.16
  (4 shorter events, 0.1 us)
Async XLA Ops:
  6.5 14.6 %copy-start.2 = (s32[16,128]{1,0:T(8,128)S(1)}, s32[16,128]{1,0:T(8,128)}, u32[]{:S(2)}) copy-start(s32[16,128]{1,0:T(8,128)} %param.4) | copy-start | bytes 24580
  6.5 362.0 %all-reduce.3.cloned.1.call-start = ((), (), s32[]{:S(2)}) async-start(), calls=%async_computation | async-start | bytes 4194304 | tf_op jit(solution)/shard_map/psum | solution.py:66
  12.6 3.3 copy-start.1
  16.0 15.0 %collective-permute-start = (f32[1024,1,128]{2,0,1:T(8,128)S(1)}, f32[1024,1,128]{2,0,1:T(8,128)S(1)}, u32[]{:S(2)}, u32[]{:S(2)}) collective-permute-start(f32[1024,1,128]{2,0,1:T(8,128)S(1)} %get-tuple-element.11), channel_id=1, source_target_pairs={{0,8},{8,16},{16,24},{24,32},{32,40},{40,48},{48,56},{56,64},{64,7... | collective-permute-start | bytes 1572872 | tf_op jit(solution)/shard_map/ppermute | solution.py:23
  19.9 17.0 %collective-permute-start.1 = (f32[1024,1,128]{2,0,1:T(8,128)S(1)}, f32[1024,1,128]{2,0,1:T(8,128)S(1)}, u32[]{:S(2)}, u32[]{:S(2)}) collective-permute-start(f32[1024,1,128]{2,0,1:T(8,128)S(1)} %get-tuple-element.10), channel_id=1, source_target_pairs={{8,0},{16,8},{24,16},{32,24},{40,32},{48,40},{56,48},{64,56},{72,6... | collective-permute-start | bytes 1572872 | tf_op jit(solution)/shard_map/ppermute | solution.py:24
  36.9 9.3 %copy-start = (f32[1024,18,128]{2,0,1:T(8,128)}, f32[1024,18,128]{2,0,1:T(8,128)S(1)}, u32[]{:S(2)}) copy-start(f32[1024,18,128]{2,0,1:T(8,128)S(1)} %constant_dynamic-update-slice_fusion) | copy-start | bytes 28311556
  51.8 10.2 %collective-permute-start.2 = (f32[1024,18,1]{0,2,1:T(1,128)S(1)}, f32[1024,18,1]{0,2,1:T(1,128)S(1)}, u32[]{:S(2)}, u32[]{:S(2)}) collective-permute-start(f32[1024,18,1]{0,2,1:T(1,128)S(1)} %copy.13), channel_id=1, source_target_pairs={{1,0},{2,1},{3,2},{4,3},{5,4},{6,5},{7,6},{9,8},{10,9},{11,10},{12... | collective-permute-start | bytes 221192 | tf_op jit(solution)/shard_map/ppermute | solution.py:24
  59.3 7.8 %collective-permute-start.3 = (f32[1024,18,1]{0,2,1:T(1,128)S(1)}, f32[1024,18,1]{0,2,1:T(1,128)S(1)}, u32[]{:S(2)}, u32[]{:S(2)}) collective-permute-start(f32[1024,18,1]{0,2,1:T(1,128)S(1)} %copy.15), channel_id=1, source_target_pairs={{0,1},{1,2},{2,3},{3,4},{4,5},{5,6},{6,7},{8,9},{9,10},{10,11},{11... | collective-permute-start | bytes 221192 | tf_op jit(solution)/shard_map/ppermute | solution.py:23
Sparse Core Ops, SparseCore 0:
  98.8 269.7 all-reduce.2
where the time goes:
time: 382 us; the launch traced here: 381 us
  waiting for transfers between devices  199 us (52%)
  blocking collectives  80.3 us (21%)
  local copies, waits for them, and re-layouts  46.3 us (12%)
  other arithmetic  22 us (6%)
  between operations  14.2 us (4%)
  matrix products  10.1 us (3%)
  starting transfers between devices  9.66 us (3%)
    psum x1, waiting for transfers between devices, on_device(): lax.psum(lax.dot_general(flat_patterns, stacked, (((1,), (1,)), ((), ()))...  189 us
    psum x1, blocking collectives, on_device(): energy = lax.psum(local_energy, ('lon', 'lat'))  80.3 us
    reduce_sum x1, other arithmetic, on_device(): local_energy = jnp.sum(east_vel * east_vel + north_vel * north_vel)  18.3 us
    unnamed x9, local copies, waits for them, and re-layouts  16.1 us
    slice x3, local copies, waits for them, and re-layouts, padded_2(): initial = lax.slice_in_dim(shard, 0, width, axis=dim)  14.1 us
    ppermute x2, waiting for transfers between devices, padded_2(): before = lax.ppermute(last, axis, up)  9.8 us
    dot_general x1, matrix products, on_device(): lax.dot_general(flat_patterns, stacked, (((1,), (1,)), ((), ())), preferr...  8.1 us
  transfers between devices with their start and end apart: 5, of which 2 were waited for; matrix products, arithmetic and copies ran while one was open for 4% of the time, Pallas kernels for 0%

commit v1 on v0

--- a/solution.py
+++ b/solution.py
@@ -64,10 +64,13 @@
     flat_patterns = patterns.reshape(mode_count, 2 * lon_cells * lat_cells)
     energy = lax.psum(local_energy, ("lon", "lat"))
     totals = lax.psum(
-        lax.dot_general(
-            flat_patterns, stacked, (((1,), (1,)), ((), ())), preferred_element_type=jnp.float32
+        lax.psum(
+            lax.dot_general(
+                flat_patterns, stacked, (((1,), (1,)), ((), ())), preferred_element_type=jnp.float32
+            ),
+            "lat",
         ),
-        ("lon", "lat"),
+        "lon",
     )
     cell_total = 2.0 * days * lon_cells * lon_devices * total_rows
     centered = totals - jnp.mean(totals, axis=1, keepdims=True)

time: 382 us -> 346 us (0.906)
  waiting for transfers between devices: 199 us -> 165 us
    psum x1, waiting for transfers between devices: 189 us -> 73.7 us  [on_device(): lax.psum(lax.dot_general(flat_patterns, stacked, (((1,), (1,)), ((), ()))...]
    psum x0 -> x1, waiting for transfers between devices: none -> 81.4 us  [on_device(): lax.psum(lax.psum(lax.dot_general(flat_patterns, stacked, (((1,), (1,)),...]
  transfers between devices with their start and end apart: 5 -> 6, of which waited for: 2 -> 3; matrix products, arithmetic and copies ran while one was open for 4% -> 5% of each run, Pallas kernels for 0% -> 0%
where the time goes in v1:
time: 346 us; the launch traced here: 345 us
  waiting for transfers between devices  165 us (48%)
  blocking collectives  78.2 us (23%)
  local copies, waits for them, and re-layouts  46.3 us (13%)
  other arithmetic  22 us (6%)
  between operations  14.2 us (4%)
  matrix products  10.1 us (3%)
  starting transfers between devices  9.7 us (3%)
    psum x1, waiting for transfers between devices, on_device(): lax.psum(lax.psum(lax.dot_general(flat_patterns, stacked, (((1,), (1,)),...  81.4 us
    psum x1, blocking collectives, on_device(): energy = lax.psum(local_energy, ('lon', 'lat'))  78.2 us
    psum x1, waiting for transfers between devices, on_device(): lax.psum(lax.dot_general(flat_patterns, stacked, (((1,), (1,)), ((), ()))...  73.7 us
    reduce_sum x1, other arithmetic, on_device(): local_energy = jnp.sum(east_vel * east_vel + north_vel * north_vel)  18.3 us
    unnamed x9, local copies, waits for them, and re-layouts  16.1 us
    slice x3, local copies, waits for them, and re-layouts, padded_2(): initial = lax.slice_in_dim(shard, 0, width, axis=dim)  14.1 us
    ppermute x2, waiting for transfers between devices, padded_2(): before = lax.ppermute(last, axis, up)  9.8 us
    dot_general x1, matrix products, on_device(): lax.dot_general(flat_patterns, stacked, (((1,), (1,)), ((), ())), preferr...  8.1 us
  transfers between devices with their start and end apart: 6, of which 3 were waited for; matrix products, arithmetic and copies ran while one was open for 5% of the time, Pallas kernels for 0%

profile of v1, /device:TPU:2, one launch (start us, length us, event | category | flops | bytes accessed | tf_op | source)
XLA Modules:
  0.0 345.5 jit_solution(9447380424828231364)
XLA Ops:
  6.5 0.0 copy-start.2
  6.5 0.0 all-reduce.4.cloned.1.call-start
  6.5 6.1 %copy.10 = f32[1024,16,128]{2,0,1:T(8,128)S(1)} copy(f32[1024,16,128]{2,1,0:T(8,128)} %param.3) | data formatting | bytes 16777216 | tf_op args[0]
  12.6 0.0 copy-start.1
  12.6 3.3 copy-done.1
  15.9 0.1 fusion.23
  16.0 3.9 %collective-permute-start = (f32[1024,1,128]{2,0,1:T(8,128)S(1)}, f32[1024,1,128]{2,0,1:T(8,128)S(1)}, u32[]{:S(2)}, u32[]{:S(2)}) collective-permute-start(f32[1024,1,128]{2,0,1:T(8,128)S(1)} %get-tuple-element.11), channel_id=1, source_target_pairs={{0,8},{8,16},{16,24},{24,32},{32,40},{40,48},{48,56},{56,64},{64,7... | collective-permute-start | bytes 1572872 | tf_op jit(solution)/shard_map/ppermute | solution.py:23
  19.9 1.3 collective-permute-start.1
  21.2 0.0 copy-done.2
  21.2 9.8 %collective-permute-done = f32[1024,1,128]{2,0,1:T(8,128)S(1)} collective-permute-done((f32[1024,1,128]{2,0,1:T(8,128)S(1)}, f32[1024,1,128]{2,0,1:T(8,128)S(1)}, u32[]{:S(2)}, u32[]{:S(2)}) %collective-permute-start) | collective-permute-done | bytes 524320 | tf_op jit(solution)/shard_map/ppermute | solution.py:23
  31.0 5.8 %constant_dynamic-update-slice_fusion.1 = f32[1024,18,128]{2,0,1:T(8,128)S(1)} fusion(f32[1024,18,128]{2,0,1:T(8,128)S(1)} %constant_dynamic-update-slice_fusion.2, f32[1024,16,128]{2,1,0:T(8,128)} %param.3), kind=kLoop, calls=%fused_computation.24 | loop fusion | bytes 16777216
  36.8 0.0 collective-permute-done.1
  36.9 0.0 copy-start
  36.9 8.4 %fusion.22 = (f32[1024,18,1]{2,0,1:T(8,128)}, f32[1024,18,1]{2,0,1:T(8,128)}) fusion(f32[1024,18,128]{2,0,1:T(8,128)S(1)} %constant_dynamic-update-slice_fusion), kind=kLoop, calls=%fused_computation.35 | loop fusion | bytes 294912 | tf_op jit(solution)/shard_map/slice | solution.py:22
  45.3 0.9 copy-done
  46.2 5.6 %copy.13 = f32[1024,18,1]{0,2,1:T(1,128)S(1)} copy(f32[1024,18,1]{2,0,1:T(8,128)} %get-tuple-element.8) | data formatting | bytes 147456 | tf_op jit(solution)/shard_map/slice | solution.py:22
  51.8 1.9 collective-permute-start.2
  53.7 5.6 %copy.15 = f32[1024,18,1]{0,2,1:T(1,128)S(1)} copy(f32[1024,18,1]{2,0,1:T(8,128)} %get-tuple-element.9) | data formatting | bytes 147456 | tf_op jit(solution)/shard_map/slice | solution.py:21
  59.3 2.6 collective-permute-start.3
  61.9 0.1 multiply_divide_fusion
  62.0 0.0 collective-permute-done.2
  62.0 5.1 %copy.14 = f32[1024,18,1]{2,0,1:T(8,128)} copy(f32[1024,18,1]{0,2,1:T(1,128)S(1)} %collective-permute-done.2) | data formatting | bytes 147456 | tf_op jit(solution)/shard_map/ppermute | solution.py:24
  67.1 0.0 collective-permute-done.3
  67.1 5.2 %copy.16 = f32[1024,18,1]{2,0,1:T(8,128)} copy(f32[1024,18,1]{0,2,1:T(1,128)S(1)} %collective-permute-done.3) | data formatting | bytes 147456 | tf_op jit(solution)/shard_map/ppermute | solution.py:23
  72.2 18.3 %add_reduce_fusion = (f32[]{:T(128)}, bf16[1024,16,128]{2,0,1:T(8,128)(2,1)S(1)}, bf16[1024,1,16,128]{3,0,2,1:T(8,128)(2,1)S(1)}) fusion(f32[16,128]{1,0:T(8,128)S(1)} %convert_element_type.18, f32[1024,16,128]{2,0,1:T(8,128)} %copy-done.1, f32[1024,1,128]{2,0,1:T(8,128)S(1)} %collective-permute-done, f32[1024,1,128]{2,0,1:T(8,128)S(1)} %collective-permute-done.1, ...), kind=kLoop, calls=%fused_computation.14 | loop fusion | flops 33554432 | bytes 27419652 | tf_op jit(solution)/shard_map/reduce_sum | solution.py:56
  90.5 8.1 %fusion.11 = f32[512,1024]{0,1:T(8,128)} fusion(bf16[512,2,16,128]{3,2,1,0:T(8,128)(2,1)} %param.5, bf16[1024,1,16,128]{3,0,2,1:T(8,128)(2,1)S(1)} %get-tuple-element.7, bf16[1024,1,16,128]{3,0,2,1:T(8,128)(2,1)S(1)} %bitcast.14), kind=kOutput, calls=%fused_computation.19 | convolution fusion | flops 4299161600 | bytes 14680064 | tf_op jit(solution)/shard_map/dot_general | solution.py:68
  98.6 0.0 all-reduce.4.cloned.1.call-update
  98.7 0.0 all-reduce.6.cloned.1.call-start
  98.7 73.7 %all-reduce.4.cloned.1.call-done = f32[512,1024]{0,1:T(8,128)} async-done(((f32[512,1024]{0,1:T(8,128)}), f32[512,1024]{0,1:T(8,128)}) %all-reduce.4.cloned.1.call-update) | async-done | bytes 2097168 | tf_op jit(solution)/shard_map/psum | solution.py:67
  172.5 0.0 all-reduce.6.cloned.1.call-update
  172.5 78.2 %psum.23 = f32[]{:T(128)} all-reduce(f32[]{:T(128)} %get-tuple-element.5), channel_id=1, replica_groups=mesh['lon'=32,'lat'=8] {'lon','lat'}, use_global_device_ids=true, to_apply=%region_4.0 | all-reduce | flops 1 | bytes 8 | tf_op jit(solution)/shard_map/psum | solution.py:65
  251.4 81.4 %all-reduce.6.cloned.1.call-done = f32[512,1024]{0,1:T(8,128)} async-done(((f32[512,1024]{0,1:T(8,128)}), f32[512,1024]{0,1:T(8,128)}) %all-reduce.6.cloned.1.call-update) | async-done | bytes 2097168 | tf_op jit(solution)/shard_map/psum | solution.py:66
  332.7 1.8 reduce_sum.18
  334.5 1.9 subtract_divide_fusion
  336.4 0.2 constant_dynamic-slice_fusion
  336.6 2.0 fusion.16
  (4 shorter events, 0.1 us)
Async XLA Ops:
  6.5 14.6 %copy-start.2 = (s32[16,128]{1,0:T(8,128)S(1)}, s32[16,128]{1,0:T(8,128)}, u32[]{:S(2)}) copy-start(s32[16,128]{1,0:T(8,128)} %param.4) | copy-start | bytes 24580
  6.5 165.9 %all-reduce.4.cloned.1.call-start = ((), (), s32[]{:S(2)}) async-start(), calls=%async_computation | async-start | bytes 4194304 | tf_op jit(solution)/shard_map/psum | solution.py:67
  12.6 3.3 copy-start.1
  16.0 15.0 %collective-permute-start = (f32[1024,1,128]{2,0,1:T(8,128)S(1)}, f32[1024,1,128]{2,0,1:T(8,128)S(1)}, u32[]{:S(2)}, u32[]{:S(2)}) collective-permute-start(f32[1024,1,128]{2,0,1:T(8,128)S(1)} %get-tuple-element.11), channel_id=1, source_target_pairs={{0,8},{8,16},{16,24},{24,32},{32,40},{40,48},{48,56},{56,64},{64,7... | collective-permute-start | bytes 1572872 | tf_op jit(solution)/shard_map/ppermute | solution.py:23
  19.9 17.0 %collective-permute-start.1 = (f32[1024,1,128]{2,0,1:T(8,128)S(1)}, f32[1024,1,128]{2,0,1:T(8,128)S(1)}, u32[]{:S(2)}, u32[]{:S(2)}) collective-permute-start(f32[1024,1,128]{2,0,1:T(8,128)S(1)} %get-tuple-element.10), channel_id=1, source_target_pairs={{8,0},{16,8},{24,16},{32,24},{40,32},{48,40},{56,48},{64,56},{72,6... | collective-permute-start | bytes 1572872 | tf_op jit(solution)/shard_map/ppermute | solution.py:24
  36.9 9.3 %copy-start = (f32[1024,18,128]{2,0,1:T(8,128)}, f32[1024,18,128]{2,0,1:T(8,128)S(1)}, u32[]{:S(2)}) copy-start(f32[1024,18,128]{2,0,1:T(8,128)S(1)} %constant_dynamic-update-slice_fusion) | copy-start | bytes 28311556
  51.8 10.2 %collective-permute-start.2 = (f32[1024,18,1]{0,2,1:T(1,128)S(1)}, f32[1024,18,1]{0,2,1:T(1,128)S(1)}, u32[]{:S(2)}, u32[]{:S(2)}) collective-permute-start(f32[1024,18,1]{0,2,1:T(1,128)S(1)} %copy.13), channel_id=1, source_target_pairs={{1,0},{2,1},{3,2},{4,3},{5,4},{6,5},{7,6},{9,8},{10,9},{11,10},{12... | collective-permute-start | bytes 221192 | tf_op jit(solution)/shard_map/ppermute | solution.py:24
  59.3 7.8 %collective-permute-start.3 = (f32[1024,18,1]{0,2,1:T(1,128)S(1)}, f32[1024,18,1]{0,2,1:T(1,128)S(1)}, u32[]{:S(2)}, u32[]{:S(2)}) collective-permute-start(f32[1024,18,1]{0,2,1:T(1,128)S(1)} %copy.15), channel_id=1, source_target_pairs={{0,1},{1,2},{2,3},{3,4},{4,5},{5,6},{6,7},{8,9},{9,10},{10,11},{11... | collective-permute-start | bytes 221192 | tf_op jit(solution)/shard_map/ppermute | solution.py:23
  98.7 234.1 %all-reduce.6.cloned.1.call-start = ((), (), s32[]{:S(2)}) async-start(), calls=%async_computation.1 | async-start | bytes 4194304 | tf_op jit(solution)/shard_map/psum | solution.py:66
Sparse Core Ops, SparseCore 0:
  98.8 73.6 all-reduce.3
  176.0 156.7 all-reduce.5
